TPU v7x, 32 devices: a whole 2x2x4 slice. The times are simulated.
32 devices in a mesh: shard: 8 (over y, x, core), rep: 4 (over z).
Axes of the slice: x: 2, y: 2, z: 4, core: 2. Of those that a mesh axis runs over, the one named last changes fastest.
Arguments:
- pooled_grad: float32 [128, 4, 8, 256], P('shard', 'rep'), may hold values from -0.8 to 0.8
- bag_lengths: int32 [8, 4, 128], P('shard', 'rep'), may hold values from 1 to 64, 2048 in all within a row
- row_slots: int32 [8, 4, 2048], P('shard', 'rep'), may hold values from 0 to 511
- id_weights: int32 [8, 4, 2048], P('shard', 'rep'), may hold values from 1 to 32
- touched_rows: float32 [8, 512, 256], P('shard'), may hold values from -6 to 6
- accumulator: float32 [8, 512], P('shard'), may hold values from 0.005 to 0.5
Outputs:
- row_grad: float32 [8, 512, 256], P('shard', 'rep')
- updated_rows: float32 [8, 512, 256], P('shard')
Inputs may be any that keep to these rules, and one draw needn't show every extreme that they name: `bag_lengths`: in each table and replica group the bag lengths sum to 2048.
All inputs are finite; a program needn't handle non-finite values.
Results may differ from a plain program's by a relative error of at most 0.0003.
Values sent between devices are 32-bit elements; how exact they have to be, the bound alone decides.
A program may use at most 64 MiB of HBM per device.

v0:
```python
import jax
import jax.numpy as jnp
from jax import lax
from jax.sharding import PartitionSpec as P

learn_rate = 0.5


def table_rows(arrived, lengths, slots, weights, height):
    ends = jnp.cumsum(lengths)
    starts = ends - lengths
    count = slots.shape[0]
    span = min(512, count)
    turns = count // span
    slot_ids = jnp.arange(height, dtype=jnp.int32)

    def add_block(step, total):
        start = step * span
        positions = start + jnp.arange(span, dtype=jnp.int32)
        target = lax.dynamic_slice_in_dim(slots, start, span)
        factor = lax.dynamic_slice_in_dim(weights, start, span)
        chosen = jnp.where(target[:, None] == slot_ids[None, :], factor[:, None], 0).astype(
            jnp.bfloat16
        )
        member = (
            (positions[:, None] >= starts[None, :]) & (positions[:, None] < ends[None, :])
        ).astype(jnp.bfloat16)
        return total + lax.dot_general(
            chosen, member, (((0,), (0,)), ((), ())), preferred_element_type=jnp.float32
        )

    empty = jnp.zeros((height, arrived.shape[0]), jnp.float32)
    tallies = lax.fori_loop(0, turns, add_block, empty)
    return (
        jnp.dot(
            tallies, arrived, precision=lax.Precision.HIGHEST, preferred_element_type=jnp.float32
        )
        * 0.0625
    )


def adagrad(rows, state, grads):
    new_state = state + jnp.mean(grads * grads, axis=-1)
    return rows - learn_rate * grads / (jnp.sqrt(new_state)[..., None] + 1e-08)


def per_device(pooled_grad, bag_lengths, row_slots, id_weights, touched_rows, accumulator):
    arrived = lax.all_to_all(pooled_grad, "shard", split_axis=2, concat_axis=0, tiled=True)
    height = touched_rows.shape[1]
    owned = touched_rows.shape[0]
    local = jnp.stack(
        [table_rows(arrived[:, 0, 0], bag_lengths[0, 0], row_slots[0, 0], id_weights[0, 0], height)]
    )
    count = height // lax.axis_size("rep")
    start = lax.axis_index("rep") * count
    grad_part = lax.psum_scatter(local, "rep", scatter_dimension=1, tiled=True)
    rows_part = lax.dynamic_slice_in_dim(touched_rows, start, count, 1)
    state_part = lax.dynamic_slice_in_dim(accumulator, start, count, 1)
    fresh = adagrad(rows_part, state_part, grad_part)
    updated = lax.all_gather(fresh, "rep", axis=1, tiled=True)
    return (grad_part, updated)


def solution(mesh):
    placed = (
        P("shard", "rep", None, None),
        P("shard", "rep", None),
        P("shard", "rep", None),
        P("shard", "rep", None),
        P("shard", None, None),
        P("shard", None),
    )
    return jax.shard_map(
        per_device,
        mesh=mesh,
        in_specs=placed,
        out_specs=(P("shard", "rep", None), P("shard", None, None)),
        check_vma=False,
    )
```

profile of v0, /device:TPU:0, one launch (start us, length us, event | category | flops | bytes accessed | tf_op | source)
XLA Modules:
  0.0 74.6 jit_solution(5423783142916893457)
XLA Ops:
  7.2 1.6 %copy.12 = f32[16,1,8,256]{3,0,1,2:T(8,128)} copy(f32[16,1,8,256]{3,2,1,0:T(8,128)} %param.8) | data formatting | bytes 262144 | tf_op args[0]
  8.8 5.2 %all-to-all-start = ((f32[16,1,8,256]{3,0,1,2:T(8,128)}), f32[16,1,8,256]{3,0,1,2:T(8,128)S(1)}, u32[]{:S(2)}, u32[]{:S(2)}) async-start(f32[16,1,8,256]{3,0,1,2:T(8,128)} %copy.12), calls=%async_computation | async-start | bytes 262144 | tf_op jit(solution)/shard_map/all_to_all | solution.py:48
  14.0 0.0 reduce-scatter.2.cloned.1.call-start
  14.0 0.0 copy-start.1
  14.0 0.6 copy-done.1
  14.7 0.1 copy.11
  14.8 0.2 reduce-window.9
  15.0 0.1 reduce.1
  15.1 8.7 %while.14 = (s32[]{:T(128)}, f32[512,128]{1,0:T(8,128)S(1)}, s32[2048]{0:T(1024)}, s32[2048]{0:T(1024)}, s32[128]{0:T(128)S(1)}, /*index=5*/s32[128]{0:T(128)S(1)}, s32[]{:T(128)}, s32[]{:T(128)}, s32[]{:T(128)}, s32[]{:T(128)}) while((s32[]{:T(128)}, f32[512,128]{1,0:T(8,128)S(1)}, s32[2048]{0:T(1024)}, s32[2048]{0:T(1024)}, ...), condition=%wide.region_2.3_spmd.clone, body=%wide.region_1.2_spmd.clone.sunk | while | flops 68223496 | bytes 541873 | solution.py:33
  15.1 0.8 %dynamic_slice.30 = s32[512]{0:T(512)S(1)} dynamic-slice(s32[2048]{0:T(1024)} %get-tuple-element.222, s32[]{:T(128)S(6)} %select_n.28), dynamic_slice_sizes={512} | dynamic-slice | bytes 4100 | tf_op jit(solution)/shard_map/while/body/eval_jaxpr/dynamic_slice | solution.py:21
  15.9 0.8 %dynamic_slice.31 = s32[512]{0:T(512)S(1)} dynamic-slice(s32[2048]{0:T(1024)} %get-tuple-element.221, s32[]{:T(128)S(6)} %select_n.28), dynamic_slice_sizes={512} | dynamic-slice | bytes 4100 | tf_op jit(solution)/shard_map/while/body/eval_jaxpr/dynamic_slice | solution.py:20
  16.6 0.6 convolution_add_fusion.2
  17.3 0.8 %dynamic_slice.30 = s32[512]{0:T(512)S(1)} dynamic-slice(s32[2048]{0:T(1024)} %get-tuple-element.222, s32[]{:T(128)S(6)} %select_n.28), dynamic_slice_sizes={512} | dynamic-slice | bytes 4100 | tf_op jit(solution)/shard_map/while/body/eval_jaxpr/dynamic_slice | solution.py:21
  18.0 0.8 %dynamic_slice.31 = s32[512]{0:T(512)S(1)} dynamic-slice(s32[2048]{0:T(1024)} %get-tuple-element.221, s32[]{:T(128)S(6)} %select_n.28), dynamic_slice_sizes={512} | dynamic-slice | bytes 4100 | tf_op jit(solution)/shard_map/while/body/eval_jaxpr/dynamic_slice | solution.py:20
  18.8 0.6 convolution_add_fusion.2
  19.4 0.8 %dynamic_slice.30 = s32[512]{0:T(512)S(1)} dynamic-slice(s32[2048]{0:T(1024)} %get-tuple-element.222, s32[]{:T(128)S(6)} %select_n.28), dynamic_slice_sizes={512} | dynamic-slice | bytes 4100 | tf_op jit(solution)/shard_map/while/body/eval_jaxpr/dynamic_slice | solution.py:21
  20.2 0.8 %dynamic_slice.31 = s32[512]{0:T(512)S(1)} dynamic-slice(s32[2048]{0:T(1024)} %get-tuple-element.221, s32[]{:T(128)S(6)} %select_n.28), dynamic_slice_sizes={512} | dynamic-slice | bytes 4100 | tf_op jit(solution)/shard_map/while/body/eval_jaxpr/dynamic_slice | solution.py:20
  21.0 0.6 convolution_add_fusion.2
  21.6 0.8 %dynamic_slice.30 = s32[512]{0:T(512)S(1)} dynamic-slice(s32[2048]{0:T(1024)} %get-tuple-element.222, s32[]{:T(128)S(6)} %select_n.28), dynamic_slice_sizes={512} | dynamic-slice | bytes 4100 | tf_op jit(solution)/shard_map/while/body/eval_jaxpr/dynamic_slice | solution.py:21
  22.4 0.8 %dynamic_slice.31 = s32[512]{0:T(512)S(1)} dynamic-slice(s32[2048]{0:T(1024)} %get-tuple-element.221, s32[]{:T(128)S(6)} %select_n.28), dynamic_slice_sizes={512} | dynamic-slice | bytes 4100 | tf_op jit(solution)/shard_map/while/body/eval_jaxpr/dynamic_slice | solution.py:20
  23.1 0.6 convolution_add_fusion.2
  23.8 0.0 all-to-all-done
  23.8 1.4 %fusion.12 = f32[1,512,256]{2,1,0:T(8,128)} fusion(f32[512,128]{1,0:T(8,128)S(1)} %get-tuple-element.126, f32[128,256]{1,0:T(8,128)S(1)} %bitcast.24), kind=kOutput, calls=%fused_computation.16 | convolution fusion | flops 201457664 | bytes 917504 | tf_op jit(solution)/shard_map/dot_general | solution.py:35
  25.1 0.0 reduce-scatter.2.cloned.1.call-update
  25.2 23.7 %reduce-scatter.2.cloned.1.call-done = f32[1,128,256]{2,1,0:T(8,128)} async-done(((f32[1,512,256]{2,1,0:T(8,128)}), f32[1,128,256]{2,1,0:T(8,128)}) %reduce-scatter.2.cloned.1.call-update) | async-done | bytes 131088 | tf_op jit(solution)/shard_map/reduce_scatter | solution.py:56
  48.8 0.0 copy-start
  48.8 1.1 %multiply_reduce_fusion = f32[128]{0:T(128)S(1)} fusion(f32[1,128,256]{2,1,0:T(8,128)} %reduce-scatter.2.cloned.1.call-done), kind=kLoop, calls=%fused_computation.18 | loop fusion | flops 65408 | bytes 131584 | tf_op jit(solution)/shard_map/reduce_sum | solution.py:43
  49.9 0.7 fusion.15
  50.6 0.0 copy-done
  50.6 1.0 %divide_subtract_fusion = f32[1,128,256]{2,1,0:T(8,128)S(1)} fusion(f32[1,128,256]{2,1,0:T(8,128)S(1)} %copy-done, f32[1,512,256]{2,1,0:T(8,128)} %param.12, s32[]{:T(128)S(6)} %select_n.20, f32[128]{0:T(128)S(1)} %fusion.15), kind=kLoop, calls=%fused_computation.17 | loop fusion | flops 98304 | bytes 393732 | tf_op jit(solution)/shard_map/sub | solution.py:44
  51.6 15.3 %all_gather.3 = f32[1,512,256]{2,1,0:T(8,128)S(1)} all-gather(f32[1,128,256]{2,1,0:T(8,128)S(1)} %divide_subtract_fusion), channel_id=1, replica_groups=mesh['shard'=8,'rep'=4] {'rep'}, dimensions={1}, use_global_device_ids=true | all-gather | bytes 655360 | tf_op jit(solution)/shard_map/all_gather | solution.py:60
  66.9 0.8 %copy.20 = f32[1,512,256]{2,1,0:T(8,128)} copy(f32[1,512,256]{2,1,0:T(8,128)S(1)} %all_gather.3) | data formatting | bytes 1048576
  (6 shorter events, 0.0 us)
Async XLA Ops:
  8.8 15.0 %all-to-all-start = ((f32[16,1,8,256]{3,0,1,2:T(8,128)}), f32[16,1,8,256]{3,0,1,2:T(8,128)S(1)}, u32[]{:S(2)}, u32[]{:S(2)}) async-start(f32[16,1,8,256]{3,0,1,2:T(8,128)} %copy.12), calls=%async_computation | async-start | bytes 262144 | tf_op jit(solution)/shard_map/all_to_all | solution.py:48
  14.0 34.9 %reduce-scatter.2.cloned.1.call-start = ((), (), s32[]{:S(2)}) async-start(), calls=%async_computation.2 | async-start | bytes 655360 | tf_op jit(solution)/shard_map/reduce_scatter | solution.py:56
  14.0 0.7 copy-start.1
  48.8 1.8 %copy-start = (f32[1,128,256]{2,1,0:T(8,128)S(1)}, f32[1,128,256]{2,1,0:T(8,128)}, u32[]{:S(2)}) copy-start(f32[1,128,256]{2,1,0:T(8,128)} %reduce-scatter.2.cloned.1.call-done) | copy-start | bytes 393220
Sparse Core Ops, SparseCore 0:
  25.3 23.5 reduce-scatter.1
where the time goes:
time: 75.2 us; the launch traced here: 74.6 us
  waiting for transfers between devices  23.7 us (32%)
  blocking collectives  15.3 us (20%)
  between operations  14.1 us (19%)
  local copies, waits for them, and re-layouts  9.26 us (12%)
  starting transfers between devices  5.23 us (7%)
  matrix products  3.76 us (5%)
  other arithmetic  3.04 us (4%)
    reduce_scatter x1, waiting for transfers between devices, per_device(): grad_part = lax.psum_scatter(local, 'rep', scatter_dimension=1, tiled=True)  23.7 us
    all_gather x1, blocking collectives, per_device(): updated = lax.all_gather(fresh, 'rep', axis=1, tiled=True)  15.3 us
    all_to_all x1, starting transfers between devices, per_device(): lax.all_to_all(pooled_grad, 'shard', split_axis=2, concat_axis=0, tiled=T...  5.2 us
    dynamic_slice x4, local copies, waits for them, and re-layouts, add_block(): factor = lax.dynamic_slice_in_dim(weights, start, span)  3.06 us
    unnamed x6, local copies, waits for them, and re-layouts  3.05 us
    dynamic_slice x4, local copies, waits for them, and re-layouts, add_block(): target = lax.dynamic_slice_in_dim(slots, start, span)  3.04 us
    dot_general x4, matrix products, add_block(): lax.dot_general(chosen, member, (((0,), (0,)), ((), ())), preferred_eleme...  2.4 us
  transfers between devices with their start and end apart: 2, of which 1 were waited for; matrix products, arithmetic and copies ran while one was open for 12% of the time, Pallas kernels for 0%

commit v1 on v0

--- a/solution.py
+++ b/solution.py
@@ -4,6 +4,19 @@
 from jax.sharding import PartitionSpec as P
 
 learn_rate = 0.5
+
+
+def trace_the_slots(buf, where_dim, field):
+    k_now, current_arr = (buf.shape[:where_dim], buf.shape[where_dim + 1 :])
+    return jnp.moveaxis(buf.reshape(*k_now, field, -1, *current_arr), where_dim, 0)
+
+
+def connect_entries(arr_in, out_dim):
+    arr_in = jnp.moveaxis(arr_in, 0, out_dim)
+    carry = arr_in.shape
+    return arr_in.reshape(
+        *carry[:out_dim], carry[out_dim] * carry[out_dim + 1], *carry[out_dim + 2 :]
+    )
 
 
 def table_rows(arrived, lengths, slots, weights, height):
@@ -45,7 +58,22 @@
 
 
 def per_device(pooled_grad, bag_lengths, row_slots, id_weights, touched_rows, accumulator):
-    arrived = lax.all_to_all(pooled_grad, "shard", split_axis=2, concat_axis=0, tiled=True)
+
+    def tails_turn(arr, along_axis, u, s0):
+        all_values = lax.axis_size(along_axis)
+        ready, earlier = (all_values, lax.axis_index(along_axis))
+        piece_out = trace_the_slots(arr, u, ready)
+        state_next = piece_out
+        for h in range(1, ready):
+            tmp, y1 = ((earlier + h) % ready, (earlier - h) % ready)
+            oldest = lax.dynamic_index_in_dim(piece_out, tmp, 0)
+            arr_next = lax.ppermute(
+                oldest, along_axis, tuple(((q, (q + h) % ready) for q in range(ready)))
+            )
+            state_next = lax.dynamic_update_slice_in_dim(state_next, arr_next, y1, axis=0)
+        return connect_entries(state_next, s0)
+
+    arrived = tails_turn(pooled_grad, "shard", 2, s0=0)
     height = touched_rows.shape[1]
     owned = touched_rows.shape[0]
     local = jnp.stack(

time: 75.2 us -> 81.9 us (1.089)
  waiting for transfers between devices: 23.7 us -> 29.3 us
  starting transfers between devices: 5.23 us -> 6.84 us
    ppermute x0 -> x7, waiting for transfers between devices: none -> 7.89 us  [tails_turn(): lax.ppermute(oldest, along_axis, tuple(((q, (q + h) % ready) for q in ran...]
    ppermute x0 -> x7, starting transfers between devices: none -> 6.8 us  [tails_turn(): lax.ppermute(oldest, along_axis, tuple(((q, (q + h) % ready) for q in ran...]
    all_to_all x1 -> x0, starting transfers between devices: 5.2 us -> none  [per_device(): lax.all_to_all(pooled_grad, 'shard', split_axis=2, concat_axis=0, tiled=T...]
    reduce_scatter x1, waiting for transfers between devices: 23.7 us -> 21.4 us  [per_device(): grad_part = lax.psum_scatter(local, 'rep', scatter_dimension=1, tiled=True)]
    unnamed x6 -> x8, local copies, waits for them, and re-layouts: 3.05 us -> 2.26 us
  transfers between devices with their start and end apart: 2 -> 8, of which waited for: 1 -> 3; matrix products, arithmetic and copies ran while one was open for 12% -> 11% of each run, Pallas kernels for 0% -> 0%
where the time goes in v1:
time: 81.9 us; the launch traced here: 81.5 us
  waiting for transfers between devices  29.3 us (36%)
  blocking collectives  15.5 us (19%)
  between operations  14.4 us (18%)
  local copies, waits for them, and re-layouts  8.53 us (10%)
  starting transfers between devices  6.84 us (8%)
  matrix products  3.76 us (5%)
  other arithmetic  3.04 us (4%)
    reduce_scatter x1, waiting for transfers between devices, per_device(): grad_part = lax.psum_scatter(local, 'rep', scatter_dimension=1, tiled=True)  21.4 us
    all_gather x1, blocking collectives, per_device(): updated = lax.all_gather(fresh, 'rep', axis=1, tiled=True)  15.5 us
    ppermute x7, waiting for transfers between devices, tails_turn(): lax.ppermute(oldest, along_axis, tuple(((q, (q + h) % ready) for q in ran...  7.89 us
    ppermute x7, starting transfers between devices, tails_turn(): lax.ppermute(oldest, along_axis, tuple(((q, (q + h) % ready) for q in ran...  6.8 us
    dynamic_slice x4, local copies, waits for them, and re-layouts, add_block(): factor = lax.dynamic_slice_in_dim(weights, start, span)  3.06 us
    dynamic_slice x4, local copies, waits for them, and re-layouts, add_block(): target = lax.dynamic_slice_in_dim(slots, start, span)  3.04 us
    dot_general x4, matrix products, add_block(): lax.dot_general(chosen, member, (((0,), (0,)), ((), ())), preferred_eleme...  2.4 us
    unnamed x8, local copies, waits for them, and re-layouts  2.26 us
  transfers between devices with their start and end apart: 8, of which 3 were waited for; matrix products, arithmetic and copies ran while one was open for 11% of the time, Pallas kernels for 0%

profile of v1, /device:TPU:0, one launch (start us, length us, event | category | flops | bytes accessed | tf_op | source)
XLA Modules:
  0.0 81.5 jit_solution(2180782518432887381)
XLA Ops:
  7.3 0.8 copy-done.1
  8.2 3.4 %collective-permute-start.6 = (f32[1,16,1,1,256]{4,1,3,2,0:T(8,128)S(1)}, f32[1,16,1,1,256]{4,1,3,2,0:T(8,128)S(1)}, u32[]{:S(2)}, u32[]{:S(2)}) collective-permute-start(f32[1,16,1,1,256]{4,1,3,2,0:T(8,128)S(1)} %get-tuple-element.162), channel_id=1, source_target_pairs={{0,28},{4,0},{8,4},{12,8},{16,12},{20,16},{24,20},{28,24},{1,29},{... | collective-permute-start | bytes 49160 | tf_op jit(solution)/shard_map/ppermute | solution.py:70
  11.6 0.6 collective-permute-start.5
  12.2 0.3 collective-permute-start.4
  12.5 1.5 %collective-permute-start.3 = (f32[1,16,1,1,256]{4,1,3,2,0:T(8,128)S(1)}, f32[1,16,1,1,256]{4,1,3,2,0:T(8,128)S(1)}, u32[]{:S(2)}, u32[]{:S(2)}) collective-permute-start(f32[1,16,1,1,256]{4,1,3,2,0:T(8,128)S(1)} %get-tuple-element.165), channel_id=1, source_target_pairs={{0,16},{4,20},{8,24},{12,28},{16,0},{20,4},{24,8},{28,12},{1,17},{... | collective-permute-start | bytes 49160 | tf_op jit(solution)/shard_map/ppermute | solution.py:70
  14.0 0.9 %collective-permute-start = (f32[1,16,1,1,256]{4,1,3,2,0:T(8,128)S(1)}, f32[1,16,1,1,256]{4,1,3,2,0:T(8,128)S(1)}, u32[]{:S(2)}, u32[]{:S(2)}) collective-permute-start(f32[1,16,1,1,256]{4,1,3,2,0:T(8,128)S(1)} %get-tuple-element.168), channel_id=1, source_target_pairs={{0,4},{4,8},{8,12},{12,16},{16,20},{20,24},{24,28},{28,0},{1,5},{5... | collective-permute-start | bytes 49160 | tf_op jit(solution)/shard_map/ppermute | solution.py:70
  14.9 0.7 copy-done.2
  15.6 0.1 copy.11
  15.7 0.2 reduce-window.9
  15.9 0.1 reduce.1
  16.0 8.7 %while.14 = (s32[]{:T(128)}, f32[512,128]{1,0:T(8,128)S(1)}, s32[2048]{0:T(1024)}, s32[2048]{0:T(1024)}, s32[128]{0:T(128)S(1)}, /*index=5*/s32[128]{0:T(128)S(1)}, s32[]{:T(128)}, s32[]{:T(128)}, s32[]{:T(128)}, s32[]{:T(128)}) while((s32[]{:T(128)}, f32[512,128]{1,0:T(8,128)S(1)}, s32[2048]{0:T(1024)}, s32[2048]{0:T(1024)}, ...), condition=%wide.region_2.3_spmd.clone, body=%wide.region_1.2_spmd.clone.sunk | while | flops 68223496 | bytes 541873 | solution.py:46
  16.0 0.8 dynamic_slice.63
  16.8 0.8 dynamic_slice.64
  17.5 0.6 convolution_add_fusion.2
  18.2 0.8 dynamic_slice.63
  18.9 0.8 dynamic_slice.64
  19.7 0.6 convolution_add_fusion.2
  20.3 0.8 dynamic_slice.63
  21.1 0.8 dynamic_slice.64
  21.9 0.6 convolution_add_fusion.2
  22.5 0.8 dynamic_slice.63
  23.3 0.8 dynamic_slice.64
  24.0 0.6 convolution_add_fusion.2
  24.9 4.6 %collective-permute-done.1 = f32[1,16,1,1,256]{4,1,3,2,0:T(8,128)S(1)} collective-permute-done((f32[1,16,1,1,256]{4,1,3,2,0:T(8,128)S(1)}, f32[1,16,1,1,256]{4,1,3,2,0:T(8,128)S(1)}, u32[]{:S(2)}, u32[]{:S(2)}) %collective-permute-start.1) | collective-permute-done | bytes 16416 | tf_op jit(solution)/shard_map/ppermute | solution.py:70
  29.5 3.3 %collective-permute-done.2 = f32[1,16,1,1,256]{4,1,3,2,0:T(8,128)S(1)} collective-permute-done((f32[1,16,1,1,256]{4,1,3,2,0:T(8,128)S(1)}, f32[1,16,1,1,256]{4,1,3,2,0:T(8,128)S(1)}, u32[]{:S(2)}, u32[]{:S(2)}) %collective-permute-start.2) | collective-permute-done | bytes 16416 | tf_op jit(solution)/shard_map/ppermute | solution.py:70
  32.9 1.4 %fusion.12 = f32[1,512,256]{2,1,0:T(8,128)} fusion(f32[512,128]{1,0:T(8,128)S(1)} %get-tuple-element.126, f32[128,256]{1,0:T(8,128)S(1)} %bitcast.49), kind=kOutput, calls=%fused_computation.16 | convolution fusion | flops 201457664 | bytes 917504 | tf_op jit(solution)/shard_map/dot_general | solution.py:48
  34.3 21.4 %reduce-scatter.2.cloned.1.call-done = f32[1,128,256]{2,1,0:T(8,128)} async-done(((f32[1,512,256]{2,1,0:T(8,128)}), f32[1,128,256]{2,1,0:T(8,128)}) %reduce-scatter.2.cloned.1.call-update) | async-done | bytes 131088 | tf_op jit(solution)/shard_map/reduce_scatter | solution.py:84
  55.6 1.1 %multiply_reduce_fusion = f32[128]{0:T(128)S(1)} fusion(f32[1,128,256]{2,1,0:T(8,128)} %reduce-scatter.2.cloned.1.call-done), kind=kLoop, calls=%fused_computation.18 | loop fusion | flops 65408 | bytes 131584 | tf_op jit(solution)/shard_map/reduce_sum | solution.py:56
  56.7 0.7 add_bitcast_fusion
  57.4 1.0 %divide_subtract_fusion = f32[1,128,256]{2,1,0:T(8,128)S(1)} fusion(f32[1,128,256]{2,1,0:T(8,128)S(1)} %copy-done, f32[1,512,256]{2,1,0:T(8,128)} %param.12, s32[]{:T(128)S(6)} %select_n.150, f32[128]{0:T(128)S(1)} %add_bitcast_fusion), kind=kLoop, calls=%fused_computation.17 | loop fusion | flops 98304 | bytes 393732 | tf_op jit(solution)/shard_map/sub | solution.py:57
  58.4 15.5 %all_gather.3 = f32[1,512,256]{2,1,0:T(8,128)S(1)} all-gather(f32[1,128,256]{2,1,0:T(8,128)S(1)} %divide_subtract_fusion), channel_id=1, replica_groups=mesh['shard'=8,'rep'=4] {'rep'}, dimensions={1}, use_global_device_ids=true | all-gather | bytes 655360 | tf_op jit(solution)/shard_map/all_gather | solution.py:88
  73.8 0.8 copy.44
  (28 shorter events, 0.3 us)
Async XLA Ops:
  7.2 0.9 %copy-start.1 = (f32[16,1,8,256]{3,2,1,0:T(8,128)S(1)}, f32[16,1,8,256]{3,2,1,0:T(8,128)}, u32[]{:S(2)}) copy-start(f32[16,1,8,256]{3,2,1,0:T(8,128)} %param.8) | copy-start | bytes 393220
  7.2 48.4 %reduce-scatter.2.cloned.1.call-start = ((), (), s32[]{:S(2)}) async-start(), calls=%async_computation.1 | async-start | bytes 655360 | tf_op jit(solution)/shard_map/reduce_scatter | solution.py:84
  8.2 24.7 %collective-permute-start.6 = (f32[1,16,1,1,256]{4,1,3,2,0:T(8,128)S(1)}, f32[1,16,1,1,256]{4,1,3,2,0:T(8,128)S(1)}, u32[]{:S(2)}, u32[]{:S(2)}) collective-permute-start(f32[1,16,1,1,256]{4,1,3,2,0:T(8,128)S(1)} %get-tuple-element.162), channel_id=1, source_target_pairs={{0,28},{4,0},{8,4},{12,8},{16,12},{20,16},{24,20},{28,24},{1,29},{... | collective-permute-start | bytes 49160 | tf_op jit(solution)/shard_map/ppermute | solution.py:70
  11.6 21.2 %collective-permute-start.5 = (f32[1,16,1,1,256]{4,1,3,2,0:T(8,128)S(1)}, f32[1,16,1,1,256]{4,1,3,2,0:T(8,128)S(1)}, u32[]{:S(2)}, u32[]{:S(2)}) collective-permute-start(f32[1,16,1,1,256]{4,1,3,2,0:T(8,128)S(1)} %get-tuple-element.163), channel_id=1, source_target_pairs={{0,24},{4,28},{8,0},{12,4},{16,8},{20,12},{24,16},{28,20},{1,25},{... | collective-permute-start | bytes 49160 | tf_op jit(solution)/shard_map/ppermute | solution.py:70
  12.2 20.6 %collective-permute-start.4 = (f32[1,16,1,1,256]{4,1,3,2,0:T(8,128)S(1)}, f32[1,16,1,1,256]{4,1,3,2,0:T(8,128)S(1)}, u32[]{:S(2)}, u32[]{:S(2)}) collective-permute-start(f32[1,16,1,1,256]{4,1,3,2,0:T(8,128)S(1)} %get-tuple-element.164), channel_id=1, source_target_pairs={{0,20},{4,24},{8,28},{12,0},{16,4},{20,8},{24,12},{28,16},{1,21},{... | collective-permute-start | bytes 49160 | tf_op jit(solution)/shard_map/ppermute | solution.py:70
  12.5 20.3 %collective-permute-start.3 = (f32[1,16,1,1,256]{4,1,3,2,0:T(8,128)S(1)}, f32[1,16,1,1,256]{4,1,3,2,0:T(8,128)S(1)}, u32[]{:S(2)}, u32[]{:S(2)}) collective-permute-start(f32[1,16,1,1,256]{4,1,3,2,0:T(8,128)S(1)} %get-tuple-element.165), channel_id=1, source_target_pairs={{0,16},{4,20},{8,24},{12,28},{16,0},{20,4},{24,8},{28,12},{1,17},{... | collective-permute-start | bytes 49160 | tf_op jit(solution)/shard_map/ppermute | solution.py:70
  14.0 10.8 %collective-permute-start = (f32[1,16,1,1,256]{4,1,3,2,0:T(8,128)S(1)}, f32[1,16,1,1,256]{4,1,3,2,0:T(8,128)S(1)}, u32[]{:S(2)}, u32[]{:S(2)}) collective-permute-start(f32[1,16,1,1,256]{4,1,3,2,0:T(8,128)S(1)} %get-tuple-element.168), channel_id=1, source_target_pairs={{0,4},{4,8},{8,12},{12,16},{16,20},{20,24},{24,28},{28,0},{1,5},{5... | collective-permute-start | bytes 49160 | tf_op jit(solution)/shard_map/ppermute | solution.py:70
  14.9 0.7 copy-start.2
  24.8 4.7 %collective-permute-start.1 = (f32[1,16,1,1,256]{4,1,3,2,0:T(8,128)S(1)}, f32[1,16,1,1,256]{4,1,3,2,0:T(8,128)S(1)}, u32[]{:S(2)}, u32[]{:S(2)}) collective-permute-start(f32[1,16,1,1,256]{4,1,3,2,0:T(8,128)S(1)} %get-tuple-element.167), channel_id=1, source_target_pairs={{0,8},{4,12},{8,16},{12,20},{16,24},{20,28},{24,0},{28,4},{1,9},{5... | collective-permute-start | bytes 49160 | tf_op jit(solution)/shard_map/ppermute | solution.py:70
  29.5 3.3 %collective-permute-start.2 = (f32[1,16,1,1,256]{4,1,3,2,0:T(8,128)S(1)}, f32[1,16,1,1,256]{4,1,3,2,0:T(8,128)S(1)}, u32[]{:S(2)}, u32[]{:S(2)}) collective-permute-start(f32[1,16,1,1,256]{4,1,3,2,0:T(8,128)S(1)} %get-tuple-element.166), channel_id=1, source_target_pairs={{0,12},{4,16},{8,20},{12,24},{16,28},{20,0},{24,4},{28,8},{1,13},{... | collective-permute-start | bytes 49160 | tf_op jit(solution)/shard_map/ppermute | solution.py:70
  55.6 1.8 %copy-start = (f32[1,128,256]{2,1,0:T(8,128)S(1)}, f32[1,128,256]{2,1,0:T(8,128)}, u32[]{:S(2)}) copy-start(f32[1,128,256]{2,1,0:T(8,128)} %reduce-scatter.2.cloned.1.call-done) | copy-start | bytes 393220
Sparse Core Ops, SparseCore 0:
  34.4 21.1 reduce-scatter.1
